TPU v7x, 32 devices: a whole 2x2x4 slice. The times are simulated.
32 devices in a mesh: batch: 8 (over z, y), mp: 4 (over x, core).
Axes of the slice: x: 2, y: 2, z: 4, core: 2. Of those that a mesh axis runs over, the one named last changes fastest.
Arguments:
- gate_act: bfloat16 [6144, 14336], P('batch', 'mp'), may hold values from -6 to 6
- up_act: bfloat16 [6144, 14336], P('batch', 'mp'), may hold values from -6 to 6
- upstream: bfloat16 [6144, 8192], P('batch', 'mp'), may hold values from -6 to 6
- kept_index: int32 [8, 8], P('batch'), may hold values from 0 to 31, as said below
- kept_count: int32 [8], P('batch'), may hold values from 1 to 8, as said below
Outputs:
- grad_down: bfloat16 [8192, 14336], P('batch', 'mp')
Inputs may be any that keep to these rules, and one draw needn't show every extreme that they name: `kept_index`: each group's row names different candidates; only the first kept_count entries of a row are kept. `kept_count`: the counts sum to 8 * 4 over the groups, and some group keeps exactly 8.
All inputs are finite; a program needn't handle non-finite values.
Results may differ from a plain program's by a relative error of at most 0.0049.
Values may be sent and summed in bfloat16 or wider, within the bound.
A program may use at most 128 MiB of HBM per device.

v0:
```python
import math
import jax
import jax.numpy as jnp
from jax import lax
from jax.sharding import PartitionSpec as P

SEQ = 24
CAND = 32


def on_device(gate_act, up_act, upstream, kept_index, kept_count):
    groups = lax.axis_size("batch")
    share = groups // 2
    keep_most = kept_index.shape[1]
    hidden_width = gate_act.shape[1]
    model_part = upstream.shape[1]
    gate_all = gate_act.reshape(CAND, SEQ, hidden_width)
    up_all = up_act.reshape(CAND, SEQ, hidden_width)
    grad_all = upstream.reshape(CAND, SEQ, model_part)
    picked = kept_index[0]
    counts = lax.all_gather(kept_count, "batch", axis=0, tiled=True)
    starts = jnp.cumsum(counts) - counts
    myself = lax.axis_index("batch")
    targets = jnp.arange(groups, dtype=jnp.int32)
    my_slot = jnp.mod(targets - starts[myself], groups)
    present = my_slot < counts[myself]
    seq_ids = picked[jnp.minimum(my_slot, keep_most - 1)]
    hidden = (
        jax.nn.silu(gate_all[seq_ids].astype(jnp.float32)) * up_all[seq_ids].astype(jnp.float32)
    ).astype(jnp.bfloat16)
    hidden_out = jnp.where(present[:, None, None], hidden, jnp.zeros_like(hidden))
    grad_out = grad_all[seq_ids]
    hidden_in, grad_in = (
        lax.all_to_all(hidden_out, "batch", split_axis=0, concat_axis=0, tiled=True),
        lax.all_to_all(grad_out, "batch", split_axis=0, concat_axis=0, tiled=True),
    )
    arrived = jnp.mod(myself - starts, groups) < counts
    chosen = jnp.argsort(1 - arrived.astype(jnp.int32), stable=True)[:share]
    hidden_rows = hidden_in[chosen].reshape(share * SEQ, hidden_width)
    grad_rows = grad_in[chosen].reshape(share * SEQ, model_part)
    full_width = lax.all_gather(grad_rows, "mp", axis=1, tiled=True)
    columns = lax.all_to_all(full_width, "batch", split_axis=1, concat_axis=0, tiled=True)
    summed = lax.dot_general(
        columns,
        lax.all_gather(hidden_rows, "batch", axis=0, tiled=True),
        (((0,), (0,)), ((), ())),
        preferred_element_type=jnp.float32,
    )
    factor = 1.0 / math.sqrt(groups * share * SEQ)
    return (summed * factor).astype(jnp.bfloat16)


def solution(mesh):
    placed = (P("batch", "mp"), P("batch", "mp"), P("batch", "mp"), P("batch", None), P("batch"))
    return jax.shard_map(
        on_device, mesh=mesh, in_specs=placed, out_specs=P("batch", "mp"), check_vma=False
    )
```

profile of v0, /device:TPU:0, one launch (start us, length us, event | category | flops | bytes accessed | tf_op | source)
XLA Modules:
  0.0 218.1 jit_solution(4112580387159058532)
XLA Ops:
  6.5 0.0 copy-start
  7.3 1.4 dynamic-slice
  8.7 0.8 dynamic-update-slice
  9.5 13.1 %all-reduce = s32[8]{0:T(128)S(1)} all-reduce(s32[8]{0:T(128)S(1)} %dynamic-update-slice), channel_id=1, replica_groups=mesh['batch'=8,'mp'=4] {'batch'}, use_global_device_ids=true, to_apply=%add | all-reduce | flops 8 | bytes 64
  22.6 0.2 reduce-window.9
  22.8 0.6 dynamic_slice.6
  23.4 0.6 fusion.11
  23.9 1.3 gather_fusion
  25.3 0.0 copy-done
  25.3 1.5 gather_fusion.1
  26.8 4.2 %all-to-all-start = ((bf16[8,24,2048]{2,1,0:T(8,128)(2,1)}), bf16[8,24,2048]{2,1,0:T(8,128)(2,1)}, u32[]{:S(2)}, u32[]{:S(2)}) async-start(bf16[8,24,2048]{2,1,0:T(8,128)(2,1)} %gather_fusion.1), calls=%async_computation | async-start | bytes 1572864 | tf_op jit(solution)/shard_map/all_to_all | solution.py:35
  31.0 0.6 dynamic_slice.7
  31.6 4.3 %gather_fusion.4 = bf16[8,24,3584]{2,1,0:T(8,128)(2,1)} fusion(bf16[32,24,3584]{2,1,0:T(8,128)(2,1)} %bitcast.35, s32[1024]{0:T(1024)S(1)} %pad_clamp_fusion.1), kind=kCustom, calls=%fused_computation.4 | custom fusion | bytes 2752544 | tf_op jit(solution)/shard_map/gather | solution.py:29
  35.9 4.3 %gather_fusion.3 = bf16[8,24,3584]{2,1,0:T(8,128)(2,1)} fusion(bf16[32,24,3584]{2,1,0:T(8,128)(2,1)} %bitcast.36, s32[1024]{0:T(1024)S(1)} %pad_clamp_fusion.1), kind=kCustom, calls=%fused_computation.3 | custom fusion | bytes 2752544 | tf_op jit(solution)/shard_map/gather | solution.py:29
  40.2 0.9 sort.17
  41.1 1.2 fusion.7
  42.3 3.7 %fusion.5 = bf16[8,24,3584]{2,1,0:T(8,128)(2,1)} fusion(bf16[8,24,3584]{2,1,0:T(8,128)(2,1)} %gather_fusion.4, bf16[8,24,3584]{2,1,0:T(8,128)(2,1)} %gather_fusion.3, pred[8]{0:T(512)(128)(4,1)S(1)} %fusion.7), kind=kLoop, calls=%fused_computation.15 | loop fusion | flops 6193152 | bytes 4128776 | tf_op jit(solution)/shard_map/jit(_where)/select_n | solution.py:31
  46.1 2.6 %all-to-all-done = bf16[8,24,2048]{2,1,0:T(8,128)(2,1)} async-done(((bf16[8,24,2048]{2,1,0:T(8,128)(2,1)}), bf16[8,24,2048]{2,1,0:T(8,128)(2,1)}, u32[]{:S(2)}, u32[]{:S(2)}) %all-to-all-start) | async-done | bytes 786464 | tf_op jit(solution)/shard_map/all_to_all | solution.py:35
  48.6 4.3 %all-to-all-start.2 = ((bf16[8,24,3584]{2,1,0:T(8,128)(2,1)}), bf16[8,24,3584]{2,1,0:T(8,128)(2,1)}, u32[]{:S(2)}, u32[]{:S(2)}) async-start(bf16[8,24,3584]{2,1,0:T(8,128)(2,1)} %fusion.5), calls=%async_computation.2 | async-start | bytes 2752512 | tf_op jit(solution)/shard_map/all_to_all | solution.py:34
  52.9 0.0 all-gather.3.cloned.1.call-start
  53.0 2.5 %gather_fusion.2 = bf16[4,24,2048]{2,1,0:T(8,128)(2,1)} fusion(bf16[8,24,2048]{2,1,0:T(8,128)(2,1)} %all-to-all-done, s32[1024]{0:T(1024)S(1)} %pad_clamp_fusion), kind=kCustom, calls=%fused_computation.2 | custom fusion | bytes 786448 | tf_op jit(solution)/shard_map/gather | solution.py:40
  55.4 0.0 all-gather.3.cloned.1.call-update
  55.5 0.0 all-gather.5.cloned.1.call-start
  55.5 28.7 %all-to-all-done.2 = bf16[8,24,3584]{2,1,0:T(8,128)(2,1)} async-done(((bf16[8,24,3584]{2,1,0:T(8,128)(2,1)}), bf16[8,24,3584]{2,1,0:T(8,128)(2,1)}, u32[]{:S(2)}, u32[]{:S(2)}) %all-to-all-start.2) | async-done | bytes 1376288 | tf_op jit(solution)/shard_map/all_to_all | solution.py:34
  84.2 2.8 %gather_fusion.5 = bf16[4,24,3584]{2,1,0:T(8,128)(2,1)} fusion(bf16[8,24,3584]{2,1,0:T(8,128)(2,1)} %all-to-all-done.2, s32[1024]{0:T(1024)S(1)} %pad_clamp_fusion), kind=kCustom, calls=%fused_computation.5 | custom fusion | bytes 1376272 | tf_op jit(solution)/shard_map/gather | solution.py:39
  87.0 0.0 all-gather.5.cloned.1.call-update
  87.0 0.0 all-gather.3.cloned.1.call-done
  87.0 1.5 copy.10
  88.6 62.6 %all_to_all.29 = bf16[96,8,1024]{2,0,1:T(8,128)(2,1)} all-to-all(bf16[96,8,1024]{2,0,1:T(8,128)(2,1)S(1)} %bitcast.30), channel_id=1, replica_groups=mesh['batch'=8,'mp'=4] {'batch'}, dimensions={1} | all-to-all | bytes 3145728 | tf_op jit(solution)/shard_map/all_to_all | solution.py:42
  151.2 49.8 %all-gather.5.cloned.1.call-done = bf16[768,3584]{1,0:T(8,128)(2,1)} async-done(((bf16[96,3584]{1,0:T(8,128)(2,1)}), bf16[768,3584]{1,0:T(8,128)(2,1)}) %all-gather.5.cloned.1.call-update) | async-done | bytes 5505040 | tf_op jit(solution)/shard_map/all_gather | solution.py:45
  201.0 10.2 %multiply_convert_fusion = bf16[1024,3584]{1,0:T(8,128)(2,1)} fusion(bf16[768,1024]{1,0:T(8,128)(2,1)} %bitcast.33, bf16[768,3584]{1,0:T(8,128)(2,1)} %all-gather.5.cloned.1.call-done), kind=kOutput, calls=%fused_computation.6 | convolution fusion | flops 5644484608 | bytes 14417920 | tf_op jit(solution)/shard_map/dot_general | solution.py:43
  (8 shorter events, 0.1 us)
Async XLA Ops:
  6.5 18.7 %copy-start = (bf16[768,2048]{1,0:T(8,128)(2,1)S(1)}, bf16[768,2048]{1,0:T(8,128)(2,1)}, u32[]{:S(2)}) copy-start(bf16[768,2048]{1,0:T(8,128)(2,1)} %param.7) | copy-start | bytes 9437188
  26.8 21.9 %all-to-all-start = ((bf16[8,24,2048]{2,1,0:T(8,128)(2,1)}), bf16[8,24,2048]{2,1,0:T(8,128)(2,1)}, u32[]{:S(2)}, u32[]{:S(2)}) async-start(bf16[8,24,2048]{2,1,0:T(8,128)(2,1)} %gather_fusion.1), calls=%async_computation | async-start | bytes 1572864 | tf_op jit(solution)/shard_map/all_to_all | solution.py:35
  48.6 35.6 %all-to-all-start.2 = ((bf16[8,24,3584]{2,1,0:T(8,128)(2,1)}), bf16[8,24,3584]{2,1,0:T(8,128)(2,1)}, u32[]{:S(2)}, u32[]{:S(2)}) async-start(bf16[8,24,3584]{2,1,0:T(8,128)(2,1)} %fusion.5), calls=%async_computation.2 | async-start | bytes 2752512 | tf_op jit(solution)/shard_map/all_to_all | solution.py:34
  52.9 34.1 %all-gather.3.cloned.1.call-start = ((), (), s32[]{:S(2)}) async-start(), calls=%async_computation.3 | async-start | bytes 1966080 | tf_op jit(solution)/shard_map/all_gather | solution.py:41
  55.5 145.6 %all-gather.5.cloned.1.call-start = ((), (), s32[]{:S(2)}) async-start(), calls=%async_computation.4 | async-start | bytes 6193152 | tf_op jit(solution)/shard_map/all_gather | solution.py:45
Sparse Core Ops, SparseCore 0:
  55.6 20.8 all-gather.2
  87.1 113.8 all-gather.4
where the time goes:
time: 219 us; the launch traced here: 218 us
  waiting for transfers between devices  81.2 us (37%)
  blocking collectives  75.7 us (35%)
  local copies, waits for them, and re-layouts  21.5 us (10%)
  between operations  14.3 us (7%)
  matrix products  10.2 us (5%)
  starting transfers between devices  8.57 us (4%)
  other arithmetic  6.7 us (3%)
    all_to_all x1, blocking collectives, on_device(): lax.all_to_all(full_width, 'batch', split_axis=1, concat_axis=0, tiled=True)  62.6 us
    all_gather x1, waiting for transfers between devices, on_device(): lax.all_gather(hidden_rows, 'batch', axis=0, tiled=True)  49.8 us
    all_to_all x1, waiting for transfers between devices, on_device(): lax.all_to_all(hidden_out, 'batch', split_axis=0, concat_axis=0, tiled=True)  28.7 us
    unnamed x1, blocking collectives  13.1 us
    dot_general x1, matrix products, on_device(): lax.dot_general(columns, lax.all_gather(hidden_rows, 'batch', axis=0, til...  10.2 us
  transfers between devices with their start and end apart: 4, of which 3 were waited for; matrix products, arithmetic and copies ran while one was open for 10% of the time, Pallas kernels for 0%

commit v1 on v0

--- a/solution.py
+++ b/solution.py
@@ -42,7 +42,9 @@
     columns = lax.all_to_all(full_width, "batch", split_axis=1, concat_axis=0, tiled=True)
     summed = lax.dot_general(
         columns,
-        lax.all_gather(hidden_rows, "batch", axis=0, tiled=True),
+        jnp.concatenate(
+            lax.all_to_all(jnp.stack([hidden_rows] * lax.axis_size("batch")), "batch", 0, 0), axis=0
+        ),
         (((0,), (0,)), ((), ())),
         preferred_element_type=jnp.float32,
     )

time: 219 us -> 268 us (1.22)
  blocking collectives: 75.7 us -> 138 us
  waiting for transfers between devices: 81.2 us -> 62.1 us
  starting transfers between devices: 8.57 us -> 12.8 us
  local copies, waits for them, and re-layouts: 21.5 us -> 24.3 us
    all_to_all x1, blocking collectives: 62.6 us -> 125 us  [on_device(): lax.all_to_all(jnp.stack([hidden_rows] * lax.axis_size('batch')), 'batch'...]
    all_gather x1 -> x0, waiting for transfers between devices: 49.8 us -> none  [on_device(): lax.all_gather(hidden_rows, 'batch', axis=0, tiled=True)]
    all_to_all x0 -> x1, waiting for transfers between devices: none -> 33.6 us  [on_device(): lax.all_to_all(full_width, 'batch', split_axis=1, concat_axis=0, tiled=True)]
    all_to_all x1, waiting for transfers between devices: 28.7 us -> 5 us  [on_device(): lax.all_to_all(hidden_out, 'batch', split_axis=0, concat_axis=0, tiled=True)]
    all_gather x1, waiting for transfers between devices: 0.02 us -> 21.1 us  [on_device(): full_width = lax.all_gather(grad_rows, 'mp', axis=1, tiled=True)]
    all_to_all x0 -> x1, starting transfers between devices: none -> 4.29 us  [on_device(): lax.all_to_all(full_width, 'batch', split_axis=1, concat_axis=0, tiled=True)]
  transfers between devices with their start and end apart: 4 -> 4, of which waited for: 3 -> 4; matrix products, arithmetic and copies ran while one was open for 10% -> 9% of each run, Pallas kernels for 0% -> 0%
where the time goes in v1:
time: 268 us
  blocking collectives  138 us (51%)
  waiting for transfers between devices  62.1 us (23%)
  local copies, waits for them, and re-layouts  24.3 us (9%)
  between operations  14.3 us (5%)
  starting transfers between devices  12.8 us (5%)
  matrix products  9.48 us (4%)
  other arithmetic  6.84 us (3%)
    all_to_all x1, blocking collectives, on_device(): lax.all_to_all(jnp.stack([hidden_rows] * lax.axis_size('batch')), 'batch'...  125 us
    all_to_all x1, waiting for transfers between devices, on_device(): lax.all_to_all(full_width, 'batch', split_axis=1, concat_axis=0, tiled=True)  33.6 us
    all_gather x1, waiting for transfers between devices, on_device(): full_width = lax.all_gather(grad_rows, 'mp', axis=1, tiled=True)  21.1 us
    unnamed x1, blocking collectives  13.1 us
    dot_general x1, matrix products, on_device(): lax.dot_general(columns, jnp.concatenate(lax.all_to_all(jnp.stack([hidden...  9.48 us
  transfers between devices with their start and end apart: 4, of which 4 were waited for; matrix products, arithmetic and copies ran while one was open for 9% of the time, Pallas kernels for 0%

profile of v1, /device:TPU:0, one launch (start us, length us, event | category | flops | bytes accessed | tf_op | source)
XLA Modules:
  0.0 267.7 jit_solution(13873027729200605351)
XLA Ops:
  6.5 0.0 copy-start
  7.3 1.4 dynamic-slice
  8.7 0.8 dynamic-update-slice
  9.5 13.1 %all-reduce = s32[8]{0:T(128)S(1)} all-reduce(s32[8]{0:T(128)S(1)} %dynamic-update-slice), channel_id=1, replica_groups=mesh['batch'=8,'mp'=4] {'batch'}, use_global_device_ids=true, to_apply=%add | all-reduce | flops 8 | bytes 64
  22.6 0.2 reduce-window.9
  22.8 0.6 dynamic_slice.6
  23.4 0.6 fusion.13
  24.0 1.3 gather_fusion
  25.3 0.0 copy-done
  25.4 1.5 gather_fusion.1
  26.9 4.2 %all-to-all-start = ((bf16[8,24,2048]{2,1,0:T(8,128)(2,1)}), bf16[8,24,2048]{2,1,0:T(8,128)(2,1)}, u32[]{:S(2)}, u32[]{:S(2)}) async-start(bf16[8,24,2048]{2,1,0:T(8,128)(2,1)} %gather_fusion.1), calls=%async_computation | async-start | bytes 1572864 | tf_op jit(solution)/shard_map/all_to_all | solution.py:35
  31.1 0.7 dynamic_slice.7
  31.7 4.3 %gather_fusion.4 = bf16[8,24,3584]{2,1,0:T(8,128)(2,1)} fusion(bf16[32,24,3584]{2,1,0:T(8,128)(2,1)} %bitcast.37, s32[1024]{0:T(1024)S(1)} %pad_clamp_fusion.1), kind=kCustom, calls=%fused_computation.4 | custom fusion | bytes 2752544 | tf_op jit(solution)/shard_map/gather | solution.py:29
  36.0 4.3 %gather_fusion.3 = bf16[8,24,3584]{2,1,0:T(8,128)(2,1)} fusion(bf16[32,24,3584]{2,1,0:T(8,128)(2,1)} %bitcast.38, s32[1024]{0:T(1024)S(1)} %pad_clamp_fusion.1), kind=kCustom, calls=%fused_computation.3 | custom fusion | bytes 2752544 | tf_op jit(solution)/shard_map/gather | solution.py:29
  40.3 1.0 sort.17
  41.3 1.3 fusion.9
  42.5 3.8 %fusion.7 = bf16[8,24,3584]{2,1,0:T(8,128)(2,1)} fusion(bf16[8,24,3584]{2,1,0:T(8,128)(2,1)} %gather_fusion.4, bf16[8,24,3584]{2,1,0:T(8,128)(2,1)} %gather_fusion.3, pred[8]{0:T(512)(128)(4,1)S(1)} %fusion.9), kind=kLoop, calls=%fused_computation.17 | loop fusion | flops 6193152 | bytes 4128776 | tf_op jit(solution)/shard_map/jit(_where)/select_n | solution.py:31
  46.3 2.4 all-to-all-done
  48.7 4.3 %all-to-all-start.2 = ((bf16[8,24,3584]{2,1,0:T(8,128)(2,1)}), bf16[8,24,3584]{2,1,0:T(8,128)(2,1)}, u32[]{:S(2)}, u32[]{:S(2)}) async-start(bf16[8,24,3584]{2,1,0:T(8,128)(2,1)} %fusion.7), calls=%async_computation.2 | async-start | bytes 2752512 | tf_op jit(solution)/shard_map/all_to_all | solution.py:34
  53.0 0.0 all-gather.2.cloned.1.call-start
  53.0 2.5 gather_fusion.2
  55.5 0.0 all-gather.2.cloned.1.call-update
  55.5 21.1 %all-gather.2.cloned.1.call-done = bf16[96,8192]{1,0:T(8,128)(2,1)} async-done(((bf16[96,2048]{1,0:T(8,128)(2,1)}), bf16[96,8192]{1,0:T(8,128)(2,1)}) %all-gather.2.cloned.1.call-update) | async-done | bytes 1572880 | tf_op jit(solution)/shard_map/all_gather | solution.py:41
  76.6 2.7 %copy.9 = bf16[12,8,8,1024]{3,2,0,1:T(8,128)(2,1)} copy(bf16[12,8,8,1024]{3,2,1,0:T(8,128)(2,1)} %bitcast.35) | data formatting | bytes 3145728 | tf_op jit(solution)/shard_map/all_to_all | solution.py:42
  79.3 5.0 %all-to-all-done.2 = bf16[8,24,3584]{2,1,0:T(8,128)(2,1)} async-done(((bf16[8,24,3584]{2,1,0:T(8,128)(2,1)}), bf16[8,24,3584]{2,1,0:T(8,128)(2,1)}, u32[]{:S(2)}, u32[]{:S(2)}) %all-to-all-start.2) | async-done | bytes 1376288 | tf_op jit(solution)/shard_map/all_to_all | solution.py:34
  84.3 4.3 %all-to-all-start.1 = ((bf16[96,8,1024]{2,0,1:T(8,128)(2,1)}), bf16[96,8,1024]{2,0,1:T(8,128)(2,1)}, u32[]{:S(2)}, u32[]{:S(2)}) async-start(bf16[96,8,1024]{2,0,1:T(8,128)(2,1)} %bitcast.33), calls=%async_computation.1 | async-start | bytes 3145728 | tf_op jit(solution)/shard_map/all_to_all | solution.py:42
  88.6 2.8 %gather_fusion.5 = bf16[4,24,3584]{2,1,0:T(8,128)(2,1)} fusion(bf16[8,24,3584]{2,1,0:T(8,128)(2,1)} %all-to-all-done.2, s32[1024]{0:T(1024)S(1)} %pad_clamp_fusion), kind=kCustom, calls=%fused_computation.5 | custom fusion | bytes 1376272 | tf_op jit(solution)/shard_map/gather | solution.py:39
  91.4 33.6 %all-to-all-done.1 = bf16[96,8,1024]{2,0,1:T(8,128)(2,1)} async-done(((bf16[96,8,1024]{2,0,1:T(8,128)(2,1)}), bf16[96,8,1024]{2,0,1:T(8,128)(2,1)}, u32[]{:S(2)}, u32[]{:S(2)}) %all-to-all-start.1) | async-done | bytes 1572896 | tf_op jit(solution)/shard_map/all_to_all | solution.py:42
  125.0 1.6 stack.3
  126.6 124.8 %all_to_all.31 = bf16[8,96,3584]{2,1,0:T(8,128)(2,1)S(1)} all-to-all(bf16[8,96,3584]{2,1,0:T(8,128)(2,1)S(1)} %stack.3), channel_id=1, replica_groups=mesh['batch'=8,'mp'=4] {'batch'}, dimensions={0} | all-to-all | bytes 11010048 | tf_op jit(solution)/shard_map/all_to_all | solution.py:46
  251.4 9.5 %fusion = bf16[1024,3584]{1,0:T(8,128)(2,1)} fusion(bf16[8,96,3584]{2,1,0:T(8,128)(2,1)S(1)} %all_to_all.31, bf16[96,8,1024]{2,0,1:T(8,128)(2,1)} %all-to-all-done.1), kind=kOutput, calls=%fused_computation.7 | convolution fusion | flops 5644484608 | bytes 14417920 | tf_op jit(solution)/shard_map/dot_general | solution.py:43
  (8 shorter events, 0.1 us)
Async XLA Ops:
  6.5 18.8 %copy-start = (bf16[768,2048]{1,0:T(8,128)(2,1)S(1)}, bf16[768,2048]{1,0:T(8,128)(2,1)}, u32[]{:S(2)}) copy-start(bf16[768,2048]{1,0:T(8,128)(2,1)} %param.7) | copy-start | bytes 9437188
  26.9 21.8 %all-to-all-start = ((bf16[8,24,2048]{2,1,0:T(8,128)(2,1)}), bf16[8,24,2048]{2,1,0:T(8,128)(2,1)}, u32[]{:S(2)}, u32[]{:S(2)}) async-start(bf16[8,24,2048]{2,1,0:T(8,128)(2,1)} %gather_fusion.1), calls=%async_computation | async-start | bytes 1572864 | tf_op jit(solution)/shard_map/all_to_all | solution.py:35
  48.7 35.6 %all-to-all-start.2 = ((bf16[8,24,3584]{2,1,0:T(8,128)(2,1)}), bf16[8,24,3584]{2,1,0:T(8,128)(2,1)}, u32[]{:S(2)}, u32[]{:S(2)}) async-start(bf16[8,24,3584]{2,1,0:T(8,128)(2,1)} %fusion.7), calls=%async_computation.2 | async-start | bytes 2752512 | tf_op jit(solution)/shard_map/all_to_all | solution.py:34
  53.0 23.6 %all-gather.2.cloned.1.call-start = ((), (), s32[]{:S(2)}) async-start(), calls=%async_computation.4 | async-start | bytes 1966080 | tf_op jit(solution)/shard_map/all_gather | solution.py:41
  84.3 40.7 %all-to-all-start.1 = ((bf16[96,8,1024]{2,0,1:T(8,128)(2,1)}), bf16[96,8,1024]{2,0,1:T(8,128)(2,1)}, u32[]{:S(2)}, u32[]{:S(2)}) async-start(bf16[96,8,1024]{2,0,1:T(8,128)(2,1)} %bitcast.33), calls=%async_computation.1 | async-start | bytes 3145728 | tf_op jit(solution)/shard_map/all_to_all | solution.py:42
Sparse Core Ops, SparseCore 0:
  55.6 20.8 all-gather.1
